TPU v7x, 32 devices: a whole 2x2x4 slice. The times are simulated.
32 devices in a mesh: dp: 16 (over z, x, core), tensor: 2 (over y).
Axes of the slice: x: 2, y: 2, z: 4, core: 2. Of those that a mesh axis runs over, the one named last changes fastest.
Arguments:
- x_input: bfloat16 [16, 768, 1536], P('dp', 'tensor'), may hold values from -6 to 6
- cond_tokens: bfloat16 [16, 130, 1536], P('dp'), may hold values from -6 to 6
- teacher: bfloat16 [16, 768, 1536], P('dp', 'tensor'), may hold values from -6 to 6
- valid_mask: int32 [16, 768], P('dp', 'tensor'), may hold values from 0 to 1, as said below
- norm_gains: bfloat16 [3, 1536], P(None, 'dp'), may hold values from 0.099609375 to 1.8984375
- w_query: bfloat16 [1536, 1536], P('dp', 'tensor'), may hold values from -0.15625 to 0.15625
- w_key: bfloat16 [1536, 1536], P('dp', 'tensor'), may hold values from -0.15625 to 0.15625
- w_value: bfloat16 [1536, 1536], P('dp', 'tensor'), may hold values from -0.15625 to 0.15625
- w_out: bfloat16 [1536, 1536], P('tensor', 'dp'), may hold values from -3 to 3
- c_query: bfloat16 [1536, 1536], P('dp', 'tensor'), may hold values from -0.15625 to 0.15625
- c_key: bfloat16 [1536, 1536], P('dp', 'tensor'), may hold values from -0.15625 to 0.15625
- c_value: bfloat16 [1536, 1536], P('dp', 'tensor'), may hold values from -0.15625 to 0.15625
- c_out: bfloat16 [1536, 1536], P('tensor', 'dp'), may hold values from -1.25 to 1.25
- w_gate: bfloat16 [1536, 6144], P('dp', 'tensor'), may hold values from -0.15625 to 0.15625
- w_up: bfloat16 [1536, 6144], P('dp', 'tensor'), may hold values from -0.15625 to 0.15625
- w_down: bfloat16 [6144, 1536], P('tensor', 'dp'), may hold values from -0.078125 to 0.078125
Outputs:
- output: bfloat16 [16, 768, 1536], P('dp', 'tensor')
- mean_loss: float32 [], replicated
- grad_input: float32 [16, 768, 1536], P('dp', 'tensor')
- grad_cond: float32 [16, 130, 1536], P('dp')
- grad_w_query: float32 [1536, 1536], P('dp', 'tensor')
- grad_w_key: float32 [1536, 1536], P('dp', 'tensor')
- grad_w_value: float32 [1536, 1536], P('dp', 'tensor')
- grad_w_out: float32 [1536, 1536], P('tensor', 'dp')
- grad_c_query: float32 [1536, 1536], P('dp', 'tensor')
- grad_c_key: float32 [1536, 1536], P('dp', 'tensor')
- grad_c_value: float32 [1536, 1536], P('dp', 'tensor')
- grad_c_out: float32 [1536, 1536], P('tensor', 'dp')
- grad_w_gate: float32 [1536, 6144], P('dp', 'tensor')
- grad_w_up: float32 [1536, 6144], P('dp', 'tensor')
- grad_w_down: float32 [6144, 1536], P('tensor', 'dp')
- grad_norm_gains: float32 [3, 1536], P(None, 'dp')
Inputs may be any that keep to these rules, and one draw needn't show every extreme that they name: `valid_mask`: the valid tokens of each latent form a prefix of it, and every latent has a valid token.
All inputs are finite; a program needn't handle non-finite values.
Results may differ from a plain program's by a relative error of at most 0.017.
Values may be sent and summed in bfloat16 or wider, within the bound.
No kernel may reach another device: no remote copies, remote signals or barrier semaphores. Data moves between devices by JAX's collectives and lax.ppermute only.
A program may use at most 256 MiB of HBM per device.

v0:
```python
import math
import jax
import jax.numpy as jnp
from jax import lax
from jax.sharding import PartitionSpec as P

HEAD_DIM = 64
EPSILON = 1e-05


def matmul(left_side, right_side):
    return jnp.dot(left_side, right_side, preferred_element_type=jnp.float32)


def contract_rows(left_side, right_side):
    return lax.dot_general(
        left_side, right_side, (((0,), (0,)), ((), ())), preferred_element_type=jnp.float32
    )


def times_transposed(left_side, right_side):
    return lax.dot_general(
        left_side, right_side, (((1,), (1,)), ((), ())), preferred_element_type=jnp.float32
    )


def norm_stats(values):
    row_mean = jnp.mean(values, axis=-1, keepdims=True)
    centred = values - row_mean
    row_var = jnp.mean(centred * centred, axis=-1, keepdims=True)
    inverse = lax.rsqrt(row_var + EPSILON)
    return (centred * inverse, inverse)


def norm_back(grad_normed, normed, inverse, gain_row):
    scaled = grad_normed * gain_row
    mean_scaled = jnp.mean(scaled, axis=-1, keepdims=True)
    mean_product = jnp.mean(scaled * normed, axis=-1, keepdims=True)
    grad_values = inverse * (scaled - mean_scaled - normed * mean_product)
    return (grad_values, jnp.sum(grad_normed * normed, axis=0))


def rotary_tables(length):
    half_dim = HEAD_DIM // 2
    freqs = jnp.exp(jnp.arange(half_dim, dtype=jnp.float32) * (-math.log(10000.0) / half_dim))
    angles = jnp.arange(length, dtype=jnp.float32)[:, None] * freqs[None, :]
    return (jnp.cos(angles)[:, None, :], jnp.sin(angles)[:, None, :])


def rotate(values, rot_cos, rot_sin):
    half_dim = HEAD_DIM // 2
    lower = values[..., :half_dim]
    upper = values[..., half_dim:]
    return jnp.concatenate(
        [lower * rot_cos - upper * rot_sin, upper * rot_cos + lower * rot_sin], axis=-1
    )


def rotate_back(values, rot_cos, rot_sin):
    half_dim = HEAD_DIM // 2
    lower = values[..., :half_dim]
    upper = values[..., half_dim:]
    return jnp.concatenate(
        [lower * rot_cos + upper * rot_sin, upper * rot_cos - lower * rot_sin], axis=-1
    )


def attend_forward(queries, keys_in, values_in):
    scale_factor = HEAD_DIM ** (-0.5)
    scores = (
        jnp.einsum("qhd,khd->hqk", queries, keys_in, preferred_element_type=jnp.float32)
        * scale_factor
    )
    row_max = jnp.max(scores, axis=-1, keepdims=True)
    shifted = jnp.exp(scores - row_max)
    row_total = jnp.sum(shifted, axis=-1, keepdims=True)
    soft_probs = (shifted / row_total).astype(jnp.bfloat16)
    mixed = jnp.einsum("hqk,khd->qhd", soft_probs, values_in, preferred_element_type=jnp.float32)
    return (mixed, row_max + jnp.log(row_total))


def attend_back(queries, keys_in, values_in, log_total, grad_mixed):
    scale_factor = HEAD_DIM ** (-0.5)
    scores = (
        jnp.einsum("qhd,khd->hqk", queries, keys_in, preferred_element_type=jnp.float32)
        * scale_factor
    )
    soft_probs = jnp.exp(scores - log_total)
    grad_values = jnp.einsum(
        "hqk,qhd->khd",
        soft_probs.astype(jnp.bfloat16),
        grad_mixed,
        preferred_element_type=jnp.float32,
    )
    grad_probs = jnp.einsum(
        "qhd,khd->hqk", grad_mixed, values_in, preferred_element_type=jnp.float32
    )
    weighted = jnp.sum(soft_probs * grad_probs, axis=-1, keepdims=True)
    grad_scores = (soft_probs * (grad_probs - weighted)).astype(jnp.bfloat16)
    grad_queries = (
        jnp.einsum("hqk,khd->qhd", grad_scores, keys_in, preferred_element_type=jnp.float32)
        * scale_factor
    )
    grad_keys = (
        jnp.einsum("hqk,qhd->khd", grad_scores, queries, preferred_element_type=jnp.float32)
        * scale_factor
    )
    return (grad_queries, grad_keys, grad_values)


def body(
    x_input,
    cond_tokens,
    teacher,
    valid_mask,
    norm_gains,
    w_query,
    w_key,
    w_value,
    w_out,
    c_query,
    c_key,
    c_value,
    c_out,
    w_gate,
    w_up,
    w_down,
):
    bf_type = jnp.bfloat16

    def fetch_attention():
        return (
            lax.all_gather(w_query, "dp", axis=0, tiled=True),
            lax.all_gather(w_key, "dp", axis=0, tiled=True),
            lax.all_gather(w_value, "dp", axis=0, tiled=True),
            lax.all_gather(w_out, "dp", axis=1, tiled=True),
            lax.all_gather(c_query, "dp", axis=0, tiled=True),
            lax.all_gather(c_key, "dp", axis=0, tiled=True),
            lax.all_gather(c_value, "dp", axis=0, tiled=True),
            lax.all_gather(c_out, "dp", axis=1, tiled=True),
            lax.all_gather(norm_gains, "dp", axis=1, tiled=True),
        )

    def fetch_mlp():
        return (
            lax.all_gather(w_gate, "dp", axis=0, tiled=True),
            lax.all_gather(w_up, "dp", axis=0, tiled=True),
            lax.all_gather(w_down, "dp", axis=1, tiled=True),
        )

    def gather_rows(values):
        return lax.all_gather(values, "tensor", axis=0, tiled=True)

    def scatter_rows(values):
        return lax.psum_scatter(values, "tensor", scatter_dimension=0, tiled=True)

    def gather_grads(values):
        return lax.all_gather(values, "tensor", axis=0, tiled=True)

    def scatter_grads(values):
        return lax.psum_scatter(values, "tensor", scatter_dimension=0, tiled=True)

    local_rows = x_input[0].astype(jnp.float32)
    cond_rows = cond_tokens[0]
    mask_float = valid_mask[0].astype(jnp.float32)
    width = local_rows.shape[1]
    token_total = float(lax.axis_size("dp") * lax.axis_size("tensor") * local_rows.shape[0])
    weight_q, weight_k, weight_v, weight_o, cross_q, cross_k, cross_v, cross_o, gains_bf = (
        fetch_attention()
    )
    gains = gains_bf.astype(jnp.float32)
    normed_one, inverse_one = norm_stats(local_rows)
    input_one = gather_rows((normed_one * gains[0]).astype(bf_type))
    length = input_one.shape[0]
    ctx_len = cond_rows.shape[0]
    rot_cos, rot_sin = rotary_tables(length)
    query_rot = rotate(
        matmul(input_one, weight_q).reshape(length, -1, HEAD_DIM), rot_cos, rot_sin
    ).astype(bf_type)
    key_rot = rotate(
        matmul(input_one, weight_k).reshape(length, -1, HEAD_DIM), rot_cos, rot_sin
    ).astype(bf_type)
    value_self = matmul(input_one, weight_v).astype(bf_type).reshape(length, -1, HEAD_DIM)
    mixed_self, log_self = attend_forward(query_rot, key_rot, value_self)
    mixed_self = mixed_self.reshape(length, -1).astype(bf_type)
    hidden_one = local_rows + scatter_rows(matmul(mixed_self, weight_o))
    normed_two, inverse_two = norm_stats(hidden_one)
    input_two = gather_rows((normed_two * gains[1]).astype(bf_type))
    query_cross = matmul(input_two, cross_q).astype(bf_type).reshape(length, -1, HEAD_DIM)
    key_cross = matmul(cond_rows, cross_k).astype(bf_type).reshape(ctx_len, -1, HEAD_DIM)
    value_cross = matmul(cond_rows, cross_v).astype(bf_type).reshape(ctx_len, -1, HEAD_DIM)
    mixed_cross, log_cross = attend_forward(query_cross, key_cross, value_cross)
    mixed_cross = mixed_cross.reshape(length, -1).astype(bf_type)
    hidden_two = hidden_one + scatter_rows(matmul(mixed_cross, cross_o))
    weight_gate, weight_up, weight_down = fetch_mlp()
    normed_three, inverse_three = norm_stats(hidden_two)
    input_three = gather_rows((normed_three * gains[2]).astype(bf_type))
    gate_pre = matmul(input_three, weight_gate)
    up_pre = matmul(input_three, weight_up)
    gate_sigmoid = jax.nn.sigmoid(gate_pre)
    gate_silu = gate_pre * gate_sigmoid
    hidden_ff = (gate_silu * up_pre).astype(bf_type)
    block_out = hidden_two + scatter_rows(matmul(hidden_ff, weight_down))
    error_diff = block_out - teacher[0].astype(jnp.float32)
    local_error = jnp.sum(mask_float[:, None] * error_diff * error_diff)
    valid_count, error_total = lax.psum((jnp.sum(mask_float), local_error), ("dp", "tensor"))
    mean_loss = error_total / (width * valid_count)
    grad_out = 2.0 * token_total / valid_count * mask_float[:, None] * error_diff
    weight_gate, weight_up, weight_down = fetch_mlp()
    branch_three = gather_grads(grad_out.astype(bf_type))
    grad_hidden = times_transposed(branch_three, weight_down)
    grad_down = contract_rows(hidden_ff, branch_three)
    grad_gate = (
        grad_hidden * up_pre * gate_sigmoid * (1.0 + gate_pre * (1.0 - gate_sigmoid))
    ).astype(bf_type)
    grad_upper = (grad_hidden * gate_silu).astype(bf_type)
    grad_gate_w = contract_rows(input_three, grad_gate)
    grad_up_w = contract_rows(input_three, grad_upper)
    grad_normed_three = scatter_grads(
        times_transposed(grad_gate, weight_gate) + times_transposed(grad_upper, weight_up)
    )
    grad_gate_s, grad_up_s, grad_down_s = (
        lax.psum_scatter(grad_gate_w, "dp", scatter_dimension=0, tiled=True),
        lax.psum_scatter(grad_up_w, "dp", scatter_dimension=0, tiled=True),
        lax.psum_scatter(grad_down, "dp", scatter_dimension=1, tiled=True),
    )
    back_three, gain_three = norm_back(grad_normed_three, normed_three, inverse_three, gains[2])
    grad_two = grad_out + back_three
    weight_q, weight_k, weight_v, weight_o, cross_q, cross_k, cross_v, cross_o, spare_gains = (
        fetch_attention()
    )
    branch_two = gather_grads(grad_two.astype(bf_type))
    grad_cross_o = contract_rows(mixed_cross, branch_two)
    grad_mixed_cross = (
        times_transposed(branch_two, cross_o).astype(bf_type).reshape(length, -1, HEAD_DIM)
    )
    grad_qc, grad_kc, grad_vc = attend_back(
        query_cross, key_cross, value_cross, log_cross, grad_mixed_cross
    )
    grad_qc = grad_qc.reshape(length, -1).astype(bf_type)
    grad_kc = grad_kc.reshape(ctx_len, -1).astype(bf_type)
    grad_vc = grad_vc.reshape(ctx_len, -1).astype(bf_type)
    grad_cross_q = contract_rows(input_two, grad_qc)
    grad_cross_k = contract_rows(cond_rows, grad_kc)
    grad_cross_v = contract_rows(cond_rows, grad_vc)
    cond_part = times_transposed(grad_kc, cross_k) + times_transposed(grad_vc, cross_v)
    grad_normed_two = scatter_grads(times_transposed(grad_qc, cross_q))
    back_two, gain_two = norm_back(grad_normed_two, normed_two, inverse_two, gains[1])
    grad_one = grad_two + back_two
    branch_one = gather_grads(grad_one.astype(bf_type))
    grad_self_o = contract_rows(mixed_self, branch_one)
    grad_mixed_self = (
        times_transposed(branch_one, weight_o).astype(bf_type).reshape(length, -1, HEAD_DIM)
    )
    grad_qs, grad_ks, grad_vs = attend_back(
        query_rot, key_rot, value_self, log_self, grad_mixed_self
    )
    grad_qs = rotate_back(grad_qs, rot_cos, rot_sin).reshape(length, -1).astype(bf_type)
    grad_ks = rotate_back(grad_ks, rot_cos, rot_sin).reshape(length, -1).astype(bf_type)
    grad_vs = grad_vs.reshape(length, -1).astype(bf_type)
    grad_self_q = contract_rows(input_one, grad_qs)
    grad_self_k = contract_rows(input_one, grad_ks)
    grad_self_v = contract_rows(input_one, grad_vs)
    grad_normed_one = scatter_grads(
        times_transposed(grad_qs, weight_q)
        + times_transposed(grad_ks, weight_k)
        + times_transposed(grad_vs, weight_v)
    )
    back_one, gain_one = norm_back(grad_normed_one, normed_one, inverse_one, gains[0])
    grad_rows = grad_one + back_one
    gain_part = jnp.stack([gain_one, gain_two, gain_three])
    cond_sum, gain_sum = (
        lax.psum(cond_part.astype(jnp.bfloat16), "tensor").astype(jnp.float32),
        lax.psum(gain_part.astype(jnp.bfloat16), "tensor").astype(jnp.float32),
    )
    (
        grad_q_s,
        grad_k_s,
        grad_v_s,
        grad_o_s,
        grad_cq_s,
        grad_ck_s,
        grad_cv_s,
        grad_co_s,
        grad_gain_s,
    ) = (
        lax.psum_scatter(grad_self_q, "dp", scatter_dimension=0, tiled=True),
        lax.psum_scatter(grad_self_k, "dp", scatter_dimension=0, tiled=True),
        lax.psum_scatter(grad_self_v, "dp", scatter_dimension=0, tiled=True),
        lax.psum_scatter(grad_self_o, "dp", scatter_dimension=1, tiled=True),
        lax.psum_scatter(grad_cross_q, "dp", scatter_dimension=0, tiled=True),
        lax.psum_scatter(grad_cross_k, "dp", scatter_dimension=0, tiled=True),
        lax.psum_scatter(grad_cross_v, "dp", scatter_dimension=0, tiled=True),
        lax.psum_scatter(grad_cross_o, "dp", scatter_dimension=1, tiled=True),
        lax.psum_scatter(gain_sum, "dp", scatter_dimension=1, tiled=True),
    )
    return (
        block_out.astype(bf_type)[None],
        mean_loss,
        grad_rows[None],
        cond_sum[None],
        grad_q_s,
        grad_k_s,
        grad_v_s,
        grad_o_s,
        grad_cq_s,
        grad_ck_s,
        grad_cv_s,
        grad_co_s,
        grad_gate_s,
        grad_up_s,
        grad_down_s,
        grad_gain_s,
    )


def solution(mesh):
    return jax.shard_map(
        body,
        mesh=mesh,
        in_specs=(
            P("dp", "tensor", None),
            P("dp", None, None),
            P("dp", "tensor", None),
            P("dp", "tensor"),
            P(None, "dp"),
            P("dp", "tensor"),
            P("dp", "tensor"),
            P("dp", "tensor"),
            P("tensor", "dp"),
            P("dp", "tensor"),
            P("dp", "tensor"),
            P("dp", "tensor"),
            P("tensor", "dp"),
            P("dp", "tensor"),
            P("dp", "tensor"),
            P("tensor", "dp"),
        ),
        out_specs=(
            P("dp", "tensor", None),
            P(),
            P("dp", "tensor", None),
            P("dp", None, None),
            P("dp", "tensor"),
            P("dp", "tensor"),
            P("dp", "tensor"),
            P("tensor", "dp"),
            P("dp", "tensor"),
            P("dp", "tensor"),
            P("dp", "tensor"),
            P("tensor", "dp"),
            P("dp", "tensor"),
            P("dp", "tensor"),
            P("tensor", "dp"),
            P(None, "dp"),
        ),
        check_vma=False,
    )
```

profile of v0, /device:TPU:0, one launch (start us, length us, event | category | flops | bytes accessed | tf_op | source)
XLA Modules:
  0.0 2735.1 jit_solution(5155967029090758559)
XLA Ops:
  10.6 23.1 all-gather
  39.1 30.3 %all-gather.19.cloned.1.call-done = bf16[768,1536]{1,0:T(8,128)(2,1)} async-done(((bf16[384,1536]{1,0:T(8,128)(2,1)}), bf16[768,1536]{1,0:T(8,128)(2,1)}) %all-gather.19.cloned.1.call-update) | async-done | bytes 2359312 | tf_op jit(solution)/shard_map/all_gather | solution.py:152
  69.5 44.6 %all-gather.25.cloned.1.call-done = bf16[1536,768]{1,0:T(8,128)(2,1)} async-done(((bf16[96,768]{1,0:T(8,128)(2,1)}), bf16[1536,768]{1,0:T(8,128)(2,1)}) %all-gather.25.cloned.1.call-update) | async-done | bytes 2359312 | tf_op jit(solution)/shard_map/all_gather | solution.py:134
  118.6 38.9 %all-gather.23.cloned.1.call-done = bf16[1536,768]{1,0:T(8,128)(2,1)} async-done(((bf16[96,768]{1,0:T(8,128)(2,1)}), bf16[1536,768]{1,0:T(8,128)(2,1)}) %all-gather.23.cloned.1.call-update) | async-done | bytes 2359312 | tf_op jit(solution)/shard_map/all_gather | solution.py:133
  174.8 12.4 fusion
  187.2 13.6 all-gather.21.cloned.1.call-done
  205.5 12.0 fusion.36
  217.5 26.6 all-gather.27.cloned.1.call-done
  252.2 56.6 %reduce-scatter.25.cloned.1.call-done = f32[384,1536]{1,0:T(8,128)} async-done(((f32[768,1536]{1,0:T(8,128)}), f32[384,1536]{1,0:T(8,128)}) %reduce-scatter.25.cloned.1.call-update) | async-done | bytes 2359312 | tf_op jit(solution)/shard_map/reduce_scatter | solution.py:155
  314.0 39.8 %all-gather.29.cloned.1.call-done = bf16[1536,768]{1,0:T(8,128)(2,1)} async-done(((bf16[96,768]{1,0:T(8,128)(2,1)}), bf16[1536,768]{1,0:T(8,128)(2,1)}) %all-gather.29.cloned.1.call-update) | async-done | bytes 2359312 | tf_op jit(solution)/shard_map/all_gather | solution.py:139
  356.9 40.6 %all-gather.35.cloned.1.call-done = bf16[1536,768]{1,0:T(8,128)(2,1)} async-done(((bf16[96,768]{1,0:T(8,128)(2,1)}), bf16[1536,768]{1,0:T(8,128)(2,1)}) %all-gather.35.cloned.1.call-update) | async-done | bytes 2359312 | tf_op jit(solution)/shard_map/all_gather | solution.py:138
  399.8 41.3 %all-gather.33.cloned.1.call-done = bf16[1536,768]{1,0:T(8,128)(2,1)} async-done(((bf16[96,768]{1,0:T(8,128)(2,1)}), bf16[1536,768]{1,0:T(8,128)(2,1)}) %all-gather.33.cloned.1.call-update) | async-done | bytes 2359312 | tf_op jit(solution)/shard_map/all_gather | solution.py:137
  441.1 36.9 %all-gather.31.cloned.1.call-done = bf16[768,1536]{1,0:T(8,128)(2,1)} async-done(((bf16[384,1536]{1,0:T(8,128)(2,1)}), bf16[768,1536]{1,0:T(8,128)(2,1)}) %all-gather.31.cloned.1.call-update) | async-done | bytes 2359312 | tf_op jit(solution)/shard_map/all_gather | solution.py:152
  488.3 34.7 %all-gather.37.cloned.1.call-done = bf16[768,1536]{0,1:T(8,128)(2,1)} async-done(((bf16[768,96]{0,1:T(8,128)(2,1)}), bf16[768,1536]{0,1:T(8,128)(2,1)}) %all-gather.37.cloned.1.call-update) | async-done | bytes 2359312 | tf_op jit(solution)/shard_map/all_gather | solution.py:140
  530.0 58.1 %reduce-scatter.27.cloned.1.call-done = f32[384,1536]{1,0:T(8,128)} async-done(((f32[768,1536]{1,0:T(8,128)}), f32[384,1536]{1,0:T(8,128)}) %reduce-scatter.27.cloned.1.call-update) | async-done | bytes 2359312 | tf_op jit(solution)/shard_map/reduce_scatter | solution.py:155
  594.5 77.3 %all-gather.41.cloned.1.call-done = bf16[1536,3072]{1,0:T(8,128)(2,1)} async-done(((bf16[96,3072]{1,0:T(8,128)(2,1)}), bf16[1536,3072]{1,0:T(8,128)(2,1)}) %all-gather.41.cloned.1.call-update) | async-done | bytes 9437200 | tf_op jit(solution)/shard_map/all_gather | solution.py:146
  671.9 36.2 %all-gather.39.cloned.1.call-done = bf16[768,1536]{1,0:T(8,128)(2,1)} async-done(((bf16[384,1536]{1,0:T(8,128)(2,1)}), bf16[768,1536]{1,0:T(8,128)(2,1)}) %all-gather.39.cloned.1.call-update) | async-done | bytes 2359312 | tf_op jit(solution)/shard_map/all_gather | solution.py:152
  708.1 14.1 fusion.64
  722.2 69.5 %all-gather.43.cloned.1.call-done = bf16[1536,3072]{1,0:T(8,128)(2,1)} async-done(((bf16[96,3072]{1,0:T(8,128)(2,1)}), bf16[1536,3072]{1,0:T(8,128)(2,1)}) %all-gather.43.cloned.1.call-update) | async-done | bytes 9437200 | tf_op jit(solution)/shard_map/all_gather | solution.py:147
  791.7 16.3 multiply_convert_fusion.3
  808.0 65.4 %all-gather.45.cloned.1.call-done = bf16[3072,1536]{0,1:T(8,128)(2,1)} async-done(((bf16[3072,96]{0,1:T(8,128)(2,1)}), bf16[3072,1536]{0,1:T(8,128)(2,1)}) %all-gather.45.cloned.1.call-update) | async-done | bytes 9437200 | tf_op jit(solution)/shard_map/all_gather | solution.py:148
  873.4 13.0 fusion.65
  887.7 39.0 %psum.29 = f32[]{:T(128)} all-reduce(f32[]{:T(128)} %get-tuple-element.93), channel_id=1, replica_groups=mesh['dp'=16,'tensor'=2] {'dp','tensor'}, use_global_device_ids=true, to_apply=%region_16.0 | all-reduce | flops 1 | bytes 8 | tf_op jit(solution)/shard_map/psum | solution.py:206
  927.4 18.7 reduce-scatter.29.cloned.1.call-done
  950.2 35.6 %all-gather.47.cloned.1.call-done = bf16[768,1536]{1,0:T(8,128)(2,1)} async-done(((bf16[384,1536]{1,0:T(8,128)(2,1)}), bf16[768,1536]{1,0:T(8,128)(2,1)}) %all-gather.47.cloned.1.call-update) | async-done | bytes 2359312 | tf_op jit(solution)/shard_map/all_gather | solution.py:158
  985.8 19.5 multiply_convert_fusion.1
  1005.3 13.1 fusion.66
  1029.3 60.1 %reduce-scatter.31.cloned.1.call-done = f32[384,1536]{1,0:T(8,128)} async-done(((f32[768,1536]{1,0:T(8,128)}), f32[384,1536]{1,0:T(8,128)}) %reduce-scatter.31.cloned.1.call-update) | async-done | bytes 2359312 | tf_op jit(solution)/shard_map/reduce_scatter | solution.py:161
  1097.9 36.0 %all-gather.49.cloned.1.call-done = bf16[768,1536]{1,0:T(8,128)(2,1)} async-done(((bf16[384,1536]{1,0:T(8,128)(2,1)}), bf16[768,1536]{1,0:T(8,128)(2,1)}) %all-gather.49.cloned.1.call-update) | async-done | bytes 2359312 | tf_op jit(solution)/shard_map/all_gather | solution.py:158
  1151.6 60.1 %reduce-scatter.33.cloned.1.call-done = f32[384,1536]{1,0:T(8,128)} async-done(((f32[768,1536]{1,0:T(8,128)}), f32[384,1536]{1,0:T(8,128)}) %reduce-scatter.33.cloned.1.call-update) | async-done | bytes 2359312 | tf_op jit(solution)/shard_map/reduce_scatter | solution.py:161
  1217.8 35.9 %all-gather.51.cloned.1.call-done = bf16[768,1536]{1,0:T(8,128)(2,1)} async-done(((bf16[384,1536]{1,0:T(8,128)(2,1)}), bf16[768,1536]{1,0:T(8,128)(2,1)}) %all-gather.51.cloned.1.call-update) | async-done | bytes 2359312 | tf_op jit(solution)/shard_map/all_gather | solution.py:158
  1270.0 22.8 multiply_reduce_fusion
  1292.8 23.9 multiply_convert_fusion
  1356.9 48.8 %reduce-scatter.35.cloned.1.call-done = f32[384,1536]{1,0:T(8,128)} async-done(((f32[768,1536]{1,0:T(8,128)}), f32[384,1536]{1,0:T(8,128)}) %reduce-scatter.35.cloned.1.call-update) | async-done | bytes 2359312 | tf_op jit(solution)/shard_map/reduce_scatter | solution.py:161
  1447.5 14.2 fusion.79
  1461.8 13.9 fusion.78
  1475.8 13.8 fusion.77
  1519.5 42.2 %psum.28 = f32[]{:T(128)} all-reduce(f32[]{:T(128)} %get-tuple-element.89), channel_id=1, replica_groups=mesh['dp'=16,'tensor'=2] {'dp','tensor'}, use_global_device_ids=true, to_apply=%region_14.0 | all-reduce | flops 1 | bytes 8 | tf_op jit(solution)/shard_map/psum | solution.py:206
  1575.0 78.9 %reduce-scatter.45.cloned.1.call-done = f32[96,768]{1,0:T(8,128)} async-done(((f32[1536,768]{1,0:T(8,128)}), f32[96,768]{1,0:T(8,128)}) %reduce-scatter.45.cloned.1.call-update) | async-done | bytes 294928 | tf_op jit(solution)/shard_map/reduce_scatter | solution.py:291
  1653.9 79.6 %reduce-scatter.57.cloned.1.call-done = f32[96,768]{1,0:T(8,128)} async-done(((f32[1536,768]{1,0:T(8,128)}), f32[96,768]{1,0:T(8,128)}) %reduce-scatter.57.cloned.1.call-update) | async-done | bytes 294928
  1733.5 79.1 %reduce-scatter.55.cloned.1.call-done = f32[96,768]{1,0:T(8,128)} async-done(((f32[1536,768]{1,0:T(8,128)}), f32[96,768]{1,0:T(8,128)}) %reduce-scatter.55.cloned.1.call-update) | async-done | bytes 294928
  1812.6 198.9 %reduce-scatter.53.cloned.1.call-done = f32[3072,96]{0,1:T(8,128)} async-done(((f32[3072,1536]{0,1:T(8,128)}), f32[3072,96]{0,1:T(8,128)}) %reduce-scatter.53.cloned.1.call-update) | async-done | bytes 1179664 | tf_op jit(solution)/shard_map/reduce_scatter | solution.py:225
  2011.5 199.2 %reduce-scatter.51.cloned.1.call-done = f32[96,3072]{1,0:T(8,128)} async-done(((f32[1536,3072]{1,0:T(8,128)}), f32[96,3072]{1,0:T(8,128)}) %reduce-scatter.51.cloned.1.call-update) | async-done | bytes 1179664 | tf_op jit(solution)/shard_map/reduce_scatter | solution.py:224
  2210.7 199.3 %reduce-scatter.49.cloned.1.call-done = f32[96,3072]{1,0:T(8,128)} async-done(((f32[1536,3072]{1,0:T(8,128)}), f32[96,3072]{1,0:T(8,128)}) %reduce-scatter.49.cloned.1.call-update) | async-done | bytes 1179664 | tf_op jit(solution)/shard_map/reduce_scatter | solution.py:223
  2410.0 79.5 %reduce-scatter.43.cloned.1.call-done = f32[768,96]{0,1:T(8,128)} async-done(((f32[768,1536]{0,1:T(8,128)}), f32[768,96]{0,1:T(8,128)}) %reduce-scatter.43.cloned.1.call-update) | async-done | bytes 294928 | tf_op jit(solution)/shard_map/reduce_scatter | solution.py:290
  2489.5 79.1 %reduce-scatter.41.cloned.1.call-done = f32[96,768]{1,0:T(8,128)} async-done(((f32[1536,768]{1,0:T(8,128)}), f32[96,768]{1,0:T(8,128)}) %reduce-scatter.41.cloned.1.call-update) | async-done | bytes 294928 | tf_op jit(solution)/shard_map/reduce_scatter | solution.py:289
  2568.5 79.6 %reduce-scatter.39.cloned.1.call-done = f32[96,768]{1,0:T(8,128)} async-done(((f32[1536,768]{1,0:T(8,128)}), f32[96,768]{1,0:T(8,128)}) %reduce-scatter.39.cloned.1.call-update) | async-done | bytes 294928 | tf_op jit(solution)/shard_map/reduce_scatter | solution.py:288
  2648.1 78.9 %reduce-scatter.37.cloned.1.call-done = f32[96,768]{1,0:T(8,128)} async-done(((f32[1536,768]{1,0:T(8,128)}), f32[96,768]{1,0:T(8,128)}) %reduce-scatter.37.cloned.1.call-update) | async-done | bytes 294928 | tf_op jit(solution)/shard_map/reduce_scatter | solution.py:287
  (318 shorter events, 265.3 us)
Async XLA Ops:
  7.2 346.6 %copy-start = (bf16[1,130,1536]{2,1,0:T(8,128)(2,1)S(1)}, bf16[1,130,1536]{2,1,0:T(8,128)(2,1)}, u32[]{:S(2)}) copy-start(bf16[1,130,1536]{2,1,0:T(8,128)(2,1)} %param.17) | copy-start | bytes 1198084
  7.2 62.3 %all-gather.19.cloned.1.call-start = ((), (), s32[]{:S(2)}) async-start(), calls=%async_computation.18 | async-start | bytes 3538944 | tf_op jit(solution)/shard_map/all_gather | solution.py:152
  10.6 108.0 %copy-start.57 = (f32[384]{0:T(512)}, f32[384]{0:T(512)S(1)}, u32[]{:S(2)}) copy-start(f32[384]{0:T(512)S(1)} %add_rsqrt_fusion.2) | copy-start | bytes 4612
  33.9 277.7 %copy-start.51 = (f32[1536]{0:T(1024)}, f32[1536]{0:T(1024)S(1)}, u32[]{:S(2)}) copy-start(f32[1536]{0:T(1024)S(1)} %get-tuple-element.91) | copy-start | bytes 18436
  35.9 78.2 %all-gather.25.cloned.1.call-start = ((), (), s32[]{:S(2)}) async-start(), calls=%async_computation.21 | async-start | bytes 2506752 | tf_op jit(solution)/shard_map/all_gather | solution.py:134
  36.7 120.8 %all-gather.23.cloned.1.call-start = ((), (), s32[]{:S(2)}) async-start(), calls=%async_computation.20 | async-start | bytes 2506752 | tf_op jit(solution)/shard_map/all_gather | solution.py:133
  37.4 163.4 %all-gather.21.cloned.1.call-start = ((), (), s32[]{:S(2)}) async-start(), calls=%async_computation.19 | async-start | bytes 2506752 | tf_op jit(solution)/shard_map/all_gather | solution.py:135
  38.0 206.1 %all-gather.27.cloned.1.call-start = ((), (), s32[]{:S(2)}) async-start(), calls=%async_computation.22 | async-start | bytes 2506752 | tf_op jit(solution)/shard_map/all_gather | solution.py:136
  38.6 270.3 %reduce-scatter.25.cloned.1.call-start = ((), (), s32[]{:S(2)}) async-start(), calls=%async_computation.23 | async-start | bytes 7077888 | tf_op jit(solution)/shard_map/reduce_scatter | solution.py:155
  39.1 123.0 %copy-start.41 = (f32[768,32]{0,1:T(8,128)}, f32[768,32]{0,1:T(8,128)S(1)}, u32[]{:S(2)}) copy-start(f32[768,32]{0,1:T(8,128)S(1)} %get-tuple-element.118) | copy-start | bytes 294916
  39.1 123.0 %copy-start.43 = (f32[768,32]{0,1:T(8,128)}, f32[768,32]{0,1:T(8,128)S(1)}, u32[]{:S(2)}) copy-start(f32[768,32]{0,1:T(8,128)S(1)} %get-tuple-element.119) | copy-start | bytes 294916
  250.0 103.8 %all-gather.29.cloned.1.call-start = ((), (), s32[]{:S(2)}) async-start(), calls=%async_computation.24 | async-start | bytes 2506752 | tf_op jit(solution)/shard_map/all_gather | solution.py:139
  250.7 146.7 %all-gather.35.cloned.1.call-start = ((), (), s32[]{:S(2)}) async-start(), calls=%async_computation.27 | async-start | bytes 2506752 | tf_op jit(solution)/shard_map/all_gather | solution.py:138
  251.5 189.7 %all-gather.33.cloned.1.call-start = ((), (), s32[]{:S(2)}) async-start(), calls=%async_computation.26 | async-start | bytes 2506752 | tf_op jit(solution)/shard_map/all_gather | solution.py:137
  252.2 225.9 %all-gather.31.cloned.1.call-start = ((), (), s32[]{:S(2)}) async-start(), calls=%async_computation.25 | async-start | bytes 3538944 | tf_op jit(solution)/shard_map/all_gather | solution.py:152
  311.2 276.9 %copy-start.2 = (f32[384,1536]{1,0:T(8,128)}, f32[384,1536]{1,0:T(8,128)S(1)}, u32[]{:S(2)}) copy-start(f32[384,1536]{1,0:T(8,128)S(1)} %get-tuple-element.102) | copy-start | bytes 7077892
  313.0 209.9 %all-gather.37.cloned.1.call-start = ((), (), s32[]{:S(2)}) async-start(), calls=%async_computation.28 | async-start | bytes 2506752 | tf_op jit(solution)/shard_map/all_gather | solution.py:140
  313.8 274.3 %reduce-scatter.27.cloned.1.call-start = ((), (), s32[]{:S(2)}) async-start(), calls=%async_computation.29 | async-start | bytes 7077888 | tf_op jit(solution)/shard_map/reduce_scatter | solution.py:155
  399.8 82.7 %copy-start.30 = (bf16[130,768]{0,1:T(8,128)(2,1)}, bf16[130,768]{0,1:T(8,128)(2,1)S(1)}, u32[]{:S(2)}) copy-start(bf16[130,768]{0,1:T(8,128)(2,1)S(1)} %copy.90) | copy-start | bytes 599044
  529.2 142.7 %all-gather.41.cloned.1.call-start = ((), (), s32[]{:S(2)}) async-start(), calls=%async_computation.31 | async-start | bytes 10027008 | tf_op jit(solution)/shard_map/all_gather | solution.py:146
  529.9 178.2 %all-gather.39.cloned.1.call-start = ((), (), s32[]{:S(2)}) async-start(), calls=%async_computation.30 | async-start | bytes 3538944 | tf_op jit(solution)/shard_map/all_gather | solution.py:152
  593.1 198.6 %all-gather.43.cloned.1.call-start = ((), (), s32[]{:S(2)}) async-start(), calls=%async_computation.32 | async-start | bytes 10027008 | tf_op jit(solution)/shard_map/all_gather | solution.py:147
  593.7 279.7 %all-gather.45.cloned.1.call-start = ((), (), s32[]{:S(2)}) async-start(), calls=%async_computation.33 | async-start | bytes 10027008 | tf_op jit(solution)/shard_map/all_gather | solution.py:148
  594.3 351.8 %reduce-scatter.29.cloned.1.call-start = ((), (), s32[]{:S(2)}) async-start(), calls=%async_computation.34 | async-start | bytes 7077888 | tf_op jit(solution)/shard_map/reduce_scatter | solution.py:155
  708.1 83.6 %copy-start.66 = (bf16[768,1536]{1,0:T(8,128)(2,1)S(1)}, bf16[768,1536]{1,0:T(8,128)(2,1)}, u32[]{:S(2)}) copy-start(bf16[768,1536]{1,0:T(8,128)(2,1)} %all-gather.39.cloned.1.call-done) | copy-start | bytes 7077892
  886.4 99.3 %all-gather.47.cloned.1.call-start = ((), (), s32[]{:S(2)}) async-start(), calls=%async_computation.35 | async-start | bytes 3538944 | tf_op jit(solution)/shard_map/all_gather | solution.py:158
  949.7 139.7 %reduce-scatter.31.cloned.1.call-start = ((), (), s32[]{:S(2)}) async-start(), calls=%async_computation.36 | async-start | bytes 7077888 | tf_op jit(solution)/shard_map/reduce_scatter | solution.py:161
  1029.3 104.6 %all-gather.49.cloned.1.call-start = ((), (), s32[]{:S(2)}) async-start(), calls=%async_computation.37 | async-start | bytes 3538944 | tf_op jit(solution)/shard_map/all_gather | solution.py:158
  1097.6 114.1 %reduce-scatter.33.cloned.1.call-start = ((), (), s32[]{:S(2)}) async-start(), calls=%async_computation.38 | async-start | bytes 7077888 | tf_op jit(solution)/shard_map/reduce_scatter | solution.py:161
  1151.5 60.2 %copy-start.52 = (f32[1536]{0:T(1024)S(1)}, f32[1536]{0:T(1024)}, u32[]{:S(2)}) copy-start(f32[1536]{0:T(1024)} %copy-done.51) | copy-start | bytes 18436
  1151.5 60.2 %copy-start.56 = (f32[384]{0:T(512)S(1)}, f32[384]{0:T(512)}, u32[]{:S(2)}) copy-start(f32[384]{0:T(512)} %copy-done.55) | copy-start | bytes 4612
  1151.5 60.2 %copy-start.60 = (f32[384]{0:T(512)S(1)}, f32[384]{0:T(512)}, u32[]{:S(2)}) copy-start(f32[384]{0:T(512)} %copy-done.59) | copy-start | bytes 4612
  1151.5 102.2 %all-gather.51.cloned.1.call-start = ((), (), s32[]{:S(2)}) async-start(), calls=%async_computation.39 | async-start | bytes 3538944 | tf_op jit(solution)/shard_map/all_gather | solution.py:158
  1217.5 188.2 %reduce-scatter.35.cloned.1.call-start = ((), (), s32[]{:S(2)}) async-start(), calls=%async_computation.40 | async-start | bytes 7077888 | tf_op jit(solution)/shard_map/reduce_scatter | solution.py:161
  1270.0 71.3 %copy-start.25 = (bf16[12,64,768]{2,1,0:T(8,128)(2,1)}, bf16[12,64,768]{2,1,0:T(8,128)(2,1)S(1)}, u32[]{:S(2)}) copy-start(bf16[12,64,768]{2,1,0:T(8,128)(2,1)S(1)} %fusion.33) | copy-start | bytes 3538948
  1345.6 216.8 %all-reduce.2.cloned.1.call-start = ((), (), s32[]{:S(2)}) async-start(), calls=%async_computation.41 | async-start | bytes 835584 | tf_op jit(solution)/shard_map/psum | solution.py:273
  1356.9 212.6 %reduce-scatter.59.cloned.1.call-start = ((), (), s32[]{:S(2)}) async-start(), calls=%async_computation.53 | async-start | bytes 835584
  1416.5 158.5 %reduce-scatter.47.cloned.1.call-start = ((), (), s32[]{:S(2)}) async-start(), calls=%async_computation.47 | async-start | bytes 5013504 | tf_op jit(solution)/shard_map/reduce_scatter | solution.py:294
  1422.8 231.1 %reduce-scatter.45.cloned.1.call-start = ((), (), s32[]{:S(2)}) async-start(), calls=%async_computation.46 | async-start | bytes 5013504 | tf_op jit(solution)/shard_map/reduce_scatter | solution.py:291
  1429.0 304.5 %reduce-scatter.57.cloned.1.call-start = ((), (), s32[]{:S(2)}) async-start(), calls=%async_computation.52 | async-start | bytes 5013504
  1438.0 374.6 %reduce-scatter.55.cloned.1.call-start = ((), (), s32[]{:S(2)}) async-start(), calls=%async_computation.51 | async-start | bytes 5013504
  1447.3 564.2 %reduce-scatter.53.cloned.1.call-start = ((), (), s32[]{:S(2)}) async-start(), calls=%async_computation.50 | async-start | bytes 20054016 | tf_op jit(solution)/shard_map/reduce_scatter | solution.py:225
  1461.8 748.9 %reduce-scatter.51.cloned.1.call-start = ((), (), s32[]{:S(2)}) async-start(), calls=%async_computation.49 | async-start | bytes 20054016 | tf_op jit(solution)/shard_map/reduce_scatter | solution.py:224
  1475.7 934.3 %reduce-scatter.49.cloned.1.call-start = ((), (), s32[]{:S(2)}) async-start(), calls=%async_computation.48 | async-start | bytes 20054016 | tf_op jit(solution)/shard_map/reduce_scatter | solution.py:223
  1489.7 999.8 %reduce-scatter.43.cloned.1.call-start = ((), (), s32[]{:S(2)}) async-start(), calls=%async_computation.45 | async-start | bytes 5013504 | tf_op jit(solution)/shard_map/reduce_scatter | solution.py:290
  1497.0 1071.5 %reduce-scatter.41.cloned.1.call-start = ((), (), s32[]{:S(2)}) async-start(), calls=%async_computation.44 | async-start | bytes 5013504 | tf_op jit(solution)/shard_map/reduce_scatter | solution.py:289
  1504.2 1143.9 %reduce-scatter.39.cloned.1.call-start = ((), (), s32[]{:S(2)}) async-start(), calls=%async_computation.43 | async-start | bytes 5013504 | tf_op jit(solution)/shard_map/reduce_scatter | solution.py:288
  1511.5 1215.5 %reduce-scatter.37.cloned.1.call-start = ((), (), s32[]{:S(2)}) async-start(), calls=%async_computation.42 | async-start | bytes 5013504 | tf_op jit(solution)/shard_map/reduce_scatter | solution.py:287
  (64 other events, 839.0 us)
Sparse Core Ops, SparseCore 0:
  36.1 33.3 all-gather.18
  71.7 42.3 all-gather.24
  116.4 41.0 all-gather.22
  159.7 41.0 all-gather.20
  202.9 41.0 all-gather.26
  250.1 58.7 reduce-scatter.24
  311.4 42.3 all-gather.28
  356.3 41.0 all-gather.34
  400.0 41.0 all-gather.32
  443.2 34.8 all-gather.30
  480.6 42.3 all-gather.36
  529.3 58.7 reduce-scatter.26
  590.4 81.4 all-gather.40
  673.8 34.1 all-gather.38
  710.2 81.4 all-gather.42
  793.8 79.5 all-gather.44
  886.5 59.5 reduce-scatter.28
  949.8 35.8 all-gather.46
  1029.4 59.9 reduce-scatter.30
  1097.7 36.0 all-gather.48
  1151.6 59.9 reduce-scatter.32
  1217.6 36.0 all-gather.50
  1345.7 59.9 reduce-scatter.34
  1408.4 26.2 all-reduce.1
  1438.3 56.7 reduce-scatter.58
  1499.8 75.1 reduce-scatter.46
  1579.3 74.5 reduce-scatter.44
  1658.8 74.6 reduce-scatter.56
  1737.9 74.6 reduce-scatter.54
  1817.7 193.8 reduce-scatter.52
  2016.8 193.8 reduce-scatter.50
  2215.9 194.0 reduce-scatter.48
  2414.8 74.6 reduce-scatter.42
  2493.9 74.5 reduce-scatter.40
  2573.5 74.5 reduce-scatter.38
  2652.4 74.5 reduce-scatter.36
where the time goes:
time: 2740 us
  waiting for transfers between devices  2170 us (79%)
  matrix products  319 us (12%)
  blocking collectives  111 us (4%)
  other arithmetic  78.4 us (3%)
  local copies, waits for them, and re-layouts  35.4 us (1%)
    reduce_scatter x1, waiting for transfers between devices, body(): lax.psum_scatter(grad_gate_w, 'dp', scatter_dimension=0, tiled=True)  199 us
    reduce_scatter x1, waiting for transfers between devices, body(): lax.psum_scatter(grad_up_w, 'dp', scatter_dimension=0, tiled=True)  199 us
    reduce_scatter x1, waiting for transfers between devices, body(): lax.psum_scatter(grad_down, 'dp', scatter_dimension=1, tiled=True)  199 us
    reduce_scatter x3, waiting for transfers between devices, scatter_grads(): return lax.psum_scatter(values, 'tensor', scatter_dimension=0, tiled=True)  169 us
    unnamed x39, waiting for transfers between devices  166 us
    reduce_scatter x3, waiting for transfers between devices, scatter_rows(): return lax.psum_scatter(values, 'tensor', scatter_dimension=0, tiled=True)  133 us
    all_gather x3, waiting for transfers between devices, gather_grads(): return lax.all_gather(values, 'tensor', axis=0, tiled=True)  107 us
    all_gather x3, waiting for transfers between devices, gather_rows(): return lax.all_gather(values, 'tensor', axis=0, tiled=True)  103 us
  transfers between devices with their start and end apart: 36, of which 34 were waited for; matrix products, arithmetic and copies ran while one was open for 8% of the time, Pallas kernels for 0%

commit v1 on v0

--- a/solution.py
+++ b/solution.py
@@ -3,9 +3,37 @@
 import jax.numpy as jnp
 from jax import lax
 from jax.sharding import PartitionSpec as P
+from jax.lax import axis_index, ppermute, psum
 
 HEAD_DIM = 64
 EPSILON = 1e-05
+
+
+def draw_ticks(array_in, out_dim):
+    array_in = jnp.moveaxis(array_in, 0, out_dim)
+    res = array_in.shape
+    v_next = array_in.reshape(*res[:out_dim], res[out_dim] * res[out_dim + 1], *res[out_dim + 2 :])
+    return v_next
+
+
+def reach_seats_all(panel, mesh_dim):
+    row_out = psum(1, axis_name=mesh_dim)
+    view_out, far_arr = (row_out, axis_index(mesh_dim))
+    passed, work_now = (panel[None], 1)
+    while work_now < view_out:
+        near = list(map(lambda hop_no: (hop_no, hop_no ^ work_now), range(view_out)))
+        part_now = ppermute(passed, mesh_dim, perm=near)
+        f_now = far_arr & work_now == 0
+        passed = jnp.concatenate(
+            [jnp.where(f_now, passed, part_now), jnp.where(f_now, part_now, passed)]
+        )
+        work_now *= 2
+    return passed
+
+
+def choose_points_for(at_axis, shard_in, u):
+    b_next = draw_ticks(reach_seats_all(u, shard_in), at_axis)
+    return b_next
 
 
 def matmul(left_side, right_side):
@@ -143,7 +171,7 @@
 
     def fetch_mlp():
         return (
-            lax.all_gather(w_gate, "dp", axis=0, tiled=True),
+            choose_points_for(0, "dp", w_gate),
             lax.all_gather(w_up, "dp", axis=0, tiled=True),
             lax.all_gather(w_down, "dp", axis=1, tiled=True),
         )

time: 2740 us -> 2900 us (1.058)
  waiting for transfers between devices: 2170 us -> 2310 us
    ppermute x0 -> x4, waiting for transfers between devices: none -> 384 us  [reach_seats_all(): part_now = ppermute(passed, mesh_dim, perm=near)]
    all_gather x1 -> x0, waiting for transfers between devices: 77.3 us -> none  [fetch_mlp(): lax.all_gather(w_gate, 'dp', axis=0, tiled=True)]
    all_gather x1, waiting for transfers between devices: 69.5 us -> 0.01 us  [fetch_mlp(): lax.all_gather(w_up, 'dp', axis=0, tiled=True)]
    all_gather x1, waiting for transfers between devices: 65.4 us -> 0.01 us  [fetch_mlp(): lax.all_gather(w_down, 'dp', axis=1, tiled=True)]
    all_gather x3, waiting for transfers between devices: 103 us -> 67.3 us  [gather_rows(): return lax.all_gather(values, 'tensor', axis=0, tiled=True)]
    unnamed x39 -> x38, waiting for transfers between devices: 166 us -> 165 us
  transfers between devices with their start and end apart: 36 -> 39, of which waited for: 34 -> 34; matrix products, arithmetic and copies ran while one was open for 8% -> 8% of each run, Pallas kernels for 0% -> 0%
where the time goes in v1:
time: 2900 us; the launch traced here: 2890 us
  waiting for transfers between devices  2310 us (80%)
  matrix products  318 us (11%)
  blocking collectives  111 us (4%)
  other arithmetic  92.7 us (3%)
  local copies, waits for them, and re-layouts  36.7 us (1%)
    ppermute x4, waiting for transfers between devices, reach_seats_all(): part_now = ppermute(passed, mesh_dim, perm=near)  384 us
    reduce_scatter x1, waiting for transfers between devices, body(): lax.psum_scatter(grad_gate_w, 'dp', scatter_dimension=0, tiled=True)  199 us
    reduce_scatter x1, waiting for transfers between devices, body(): lax.psum_scatter(grad_up_w, 'dp', scatter_dimension=0, tiled=True)  199 us
    reduce_scatter x1, waiting for transfers between devices, body(): lax.psum_scatter(grad_down, 'dp', scatter_dimension=1, tiled=True)  199 us
    reduce_scatter x3, waiting for transfers between devices, scatter_grads(): return lax.psum_scatter(values, 'tensor', scatter_dimension=0, tiled=True)  169 us
    unnamed x38, waiting for transfers between devices  165 us
    reduce_scatter x3, waiting for transfers between devices, scatter_rows(): return lax.psum_scatter(values, 'tensor', scatter_dimension=0, tiled=True)  136 us
    all_gather x3, waiting for transfers between devices, gather_grads(): return lax.all_gather(values, 'tensor', axis=0, tiled=True)  108 us
  transfers between devices with their start and end apart: 39, of which 34 were waited for; matrix products, arithmetic and copies ran while one was open for 8% of the time, Pallas kernels for 0%

profile of v1, /device:TPU:0, one launch (start us, length us, event | category | flops | bytes accessed | tf_op | source)
XLA Modules:
  0.0 2893.3 jit_solution(2558345846389660773)
XLA Ops:
  10.6 23.1 all-gather
  39.1 30.3 %all-gather.18.cloned.1.call-done = bf16[768,1536]{1,0:T(8,128)(2,1)} async-done(((bf16[384,1536]{1,0:T(8,128)(2,1)}), bf16[768,1536]{1,0:T(8,128)(2,1)}) %all-gather.18.cloned.1.call-update) | async-done | bytes 2359312 | tf_op jit(solution)/shard_map/all_gather | solution.py:180
  69.5 44.6 %all-gather.24.cloned.1.call-done = bf16[1536,768]{1,0:T(8,128)(2,1)} async-done(((bf16[96,768]{1,0:T(8,128)(2,1)}), bf16[1536,768]{1,0:T(8,128)(2,1)}) %all-gather.24.cloned.1.call-update) | async-done | bytes 2359312 | tf_op jit(solution)/shard_map/all_gather | solution.py:162
  118.6 38.9 %all-gather.22.cloned.1.call-done = bf16[1536,768]{1,0:T(8,128)(2,1)} async-done(((bf16[96,768]{1,0:T(8,128)(2,1)}), bf16[1536,768]{1,0:T(8,128)(2,1)}) %all-gather.22.cloned.1.call-update) | async-done | bytes 2359312 | tf_op jit(solution)/shard_map/all_gather | solution.py:161
  174.4 12.4 fusion
  186.8 14.0 all-gather.20.cloned.1.call-done
  205.5 11.9 fusion.36
  217.5 26.6 all-gather.26.cloned.1.call-done
  252.2 56.6 %reduce-scatter.25.cloned.1.call-done = f32[384,1536]{1,0:T(8,128)} async-done(((f32[768,1536]{1,0:T(8,128)}), f32[384,1536]{1,0:T(8,128)}) %reduce-scatter.25.cloned.1.call-update) | async-done | bytes 2359312 | tf_op jit(solution)/shard_map/reduce_scatter | solution.py:183
  314.0 39.7 %all-gather.28.cloned.1.call-done = bf16[1536,768]{1,0:T(8,128)(2,1)} async-done(((bf16[96,768]{1,0:T(8,128)(2,1)}), bf16[1536,768]{1,0:T(8,128)(2,1)}) %all-gather.28.cloned.1.call-update) | async-done | bytes 2359312 | tf_op jit(solution)/shard_map/all_gather | solution.py:167
  356.9 40.6 %all-gather.34.cloned.1.call-done = bf16[1536,768]{1,0:T(8,128)(2,1)} async-done(((bf16[96,768]{1,0:T(8,128)(2,1)}), bf16[1536,768]{1,0:T(8,128)(2,1)}) %all-gather.34.cloned.1.call-update) | async-done | bytes 2359312 | tf_op jit(solution)/shard_map/all_gather | solution.py:166
  399.8 41.3 %all-gather.32.cloned.1.call-done = bf16[1536,768]{1,0:T(8,128)(2,1)} async-done(((bf16[96,768]{1,0:T(8,128)(2,1)}), bf16[1536,768]{1,0:T(8,128)(2,1)}) %all-gather.32.cloned.1.call-update) | async-done | bytes 2359312 | tf_op jit(solution)/shard_map/all_gather | solution.py:165
  441.1 36.9 %all-gather.30.cloned.1.call-done = bf16[768,1536]{1,0:T(8,128)(2,1)} async-done(((bf16[384,1536]{1,0:T(8,128)(2,1)}), bf16[768,1536]{1,0:T(8,128)(2,1)}) %all-gather.30.cloned.1.call-update) | async-done | bytes 2359312 | tf_op jit(solution)/shard_map/all_gather | solution.py:180
  488.3 34.7 %all-gather.36.cloned.1.call-done = bf16[768,1536]{0,1:T(8,128)(2,1)} async-done(((bf16[768,96]{0,1:T(8,128)(2,1)}), bf16[768,1536]{0,1:T(8,128)(2,1)}) %all-gather.36.cloned.1.call-update) | async-done | bytes 2359312 | tf_op jit(solution)/shard_map/all_gather | solution.py:168
  529.2 58.9 %reduce-scatter.27.cloned.1.call-done = f32[384,1536]{1,0:T(8,128)} async-done(((f32[768,1536]{1,0:T(8,128)}), f32[384,1536]{1,0:T(8,128)}) %reduce-scatter.27.cloned.1.call-update) | async-done | bytes 2359312 | tf_op jit(solution)/shard_map/reduce_scatter | solution.py:183
  598.5 26.7 collective-permute-done.1
  628.3 98.6 %collective-permute-done.2 = bf16[4,96,3072]{2,1,0:T(8,128)(2,1)} collective-permute-done((bf16[4,96,3072]{2,1,0:T(8,128)(2,1)S(1)}, bf16[4,96,3072]{2,1,0:T(8,128)(2,1)}, u32[]{:S(2)}, u32[]{:S(2)}) %collective-permute-start.2) | collective-permute-done | bytes 2359328 | tf_op jit(solution)/shard_map/ppermute | solution.py:25
  736.3 257.4 %collective-permute-done.3 = bf16[8,96,3072]{2,1,0:T(8,128)(2,1)} collective-permute-done((bf16[8,96,3072]{2,1,0:T(8,128)(2,1)}, bf16[8,96,3072]{2,1,0:T(8,128)(2,1)}, u32[]{:S(2)}, u32[]{:S(2)}) %collective-permute-start.3) | collective-permute-done | bytes 4718624 | tf_op jit(solution)/shard_map/ppermute | solution.py:25
  1001.2 13.1 fusion.64
  1014.2 16.3 multiply_convert_fusion.3
  1030.5 13.1 fusion.65
  1044.9 38.3 %psum.29 = f32[]{:T(128)} all-reduce(f32[]{:T(128)} %get-tuple-element.93), channel_id=1, replica_groups=mesh['dp'=16,'tensor'=2] {'dp','tensor'}, use_global_device_ids=true, to_apply=%region_16.17 | all-reduce | flops 1 | bytes 8 | tf_op jit(solution)/shard_map/psum | solution.py:234
  1083.9 20.0 reduce-scatter.29.cloned.1.call-done
  1107.7 35.9 %all-gather.44.cloned.1.call-done = bf16[768,1536]{1,0:T(8,128)(2,1)} async-done(((bf16[384,1536]{1,0:T(8,128)(2,1)}), bf16[768,1536]{1,0:T(8,128)(2,1)}) %all-gather.44.cloned.1.call-update) | async-done | bytes 2359312 | tf_op jit(solution)/shard_map/all_gather | solution.py:186
  1143.7 19.7 multiply_convert_fusion.2
  1163.4 13.1 fusion.66
  1187.5 60.1 %reduce-scatter.31.cloned.1.call-done = f32[384,1536]{1,0:T(8,128)} async-done(((f32[768,1536]{1,0:T(8,128)}), f32[384,1536]{1,0:T(8,128)}) %reduce-scatter.31.cloned.1.call-update) | async-done | bytes 2359312 | tf_op jit(solution)/shard_map/reduce_scatter | solution.py:189
  1256.1 35.9 %all-gather.46.cloned.1.call-done = bf16[768,1536]{1,0:T(8,128)(2,1)} async-done(((bf16[384,1536]{1,0:T(8,128)(2,1)}), bf16[768,1536]{1,0:T(8,128)(2,1)}) %all-gather.46.cloned.1.call-update) | async-done | bytes 2359312 | tf_op jit(solution)/shard_map/all_gather | solution.py:186
  1309.7 60.1 %reduce-scatter.33.cloned.1.call-done = f32[384,1536]{1,0:T(8,128)} async-done(((f32[768,1536]{1,0:T(8,128)}), f32[384,1536]{1,0:T(8,128)}) %reduce-scatter.33.cloned.1.call-update) | async-done | bytes 2359312 | tf_op jit(solution)/shard_map/reduce_scatter | solution.py:189
  1376.1 35.8 %all-gather.48.cloned.1.call-done = bf16[768,1536]{1,0:T(8,128)(2,1)} async-done(((bf16[384,1536]{1,0:T(8,128)(2,1)}), bf16[768,1536]{1,0:T(8,128)(2,1)}) %all-gather.48.cloned.1.call-update) | async-done | bytes 2359312 | tf_op jit(solution)/shard_map/all_gather | solution.py:186
  1416.3 11.9 fusion.33
  1428.2 22.9 multiply_reduce_fusion
  1451.1 23.7 multiply_convert_fusion
  1515.1 48.8 %reduce-scatter.35.cloned.1.call-done = f32[384,1536]{1,0:T(8,128)} async-done(((f32[768,1536]{1,0:T(8,128)}), f32[384,1536]{1,0:T(8,128)}) %reduce-scatter.35.cloned.1.call-update) | async-done | bytes 2359312 | tf_op jit(solution)/shard_map/reduce_scatter | solution.py:189
  1605.9 14.2 fusion.79
  1620.2 13.8 fusion.77
  1634.1 13.8 fusion.78
  1677.7 42.2 %psum.28 = f32[]{:T(128)} all-reduce(f32[]{:T(128)} %get-tuple-element.89), channel_id=1, replica_groups=mesh['dp'=16,'tensor'=2] {'dp','tensor'}, use_global_device_ids=true, to_apply=%region_14.15 | all-reduce | flops 1 | bytes 8 | tf_op jit(solution)/shard_map/psum | solution.py:234
  1733.3 78.9 %reduce-scatter.45.cloned.1.call-done = f32[96,768]{1,0:T(8,128)} async-done(((f32[1536,768]{1,0:T(8,128)}), f32[96,768]{1,0:T(8,128)}) %reduce-scatter.45.cloned.1.call-update) | async-done | bytes 294928 | tf_op jit(solution)/shard_map/reduce_scatter | solution.py:319
  1812.2 79.4 %reduce-scatter.57.cloned.1.call-done = f32[96,768]{1,0:T(8,128)} async-done(((f32[1536,768]{1,0:T(8,128)}), f32[96,768]{1,0:T(8,128)}) %reduce-scatter.57.cloned.1.call-update) | async-done | bytes 294928
  1891.7 79.0 %reduce-scatter.55.cloned.1.call-done = f32[96,768]{1,0:T(8,128)} async-done(((f32[1536,768]{1,0:T(8,128)}), f32[96,768]{1,0:T(8,128)}) %reduce-scatter.55.cloned.1.call-update) | async-done | bytes 294928
  1970.7 199.1 %reduce-scatter.53.cloned.1.call-done = f32[3072,96]{0,1:T(8,128)} async-done(((f32[3072,1536]{0,1:T(8,128)}), f32[3072,96]{0,1:T(8,128)}) %reduce-scatter.53.cloned.1.call-update) | async-done | bytes 1179664 | tf_op jit(solution)/shard_map/reduce_scatter | solution.py:253
  2169.9 199.2 %reduce-scatter.49.cloned.1.call-done = f32[96,3072]{1,0:T(8,128)} async-done(((f32[1536,3072]{1,0:T(8,128)}), f32[96,3072]{1,0:T(8,128)}) %reduce-scatter.49.cloned.1.call-update) | async-done | bytes 1179664 | tf_op jit(solution)/shard_map/reduce_scatter | solution.py:251
  2369.0 199.2 %reduce-scatter.51.cloned.1.call-done = f32[96,3072]{1,0:T(8,128)} async-done(((f32[1536,3072]{1,0:T(8,128)}), f32[96,3072]{1,0:T(8,128)}) %reduce-scatter.51.cloned.1.call-update) | async-done | bytes 1179664 | tf_op jit(solution)/shard_map/reduce_scatter | solution.py:252
  2568.2 79.6 %reduce-scatter.43.cloned.1.call-done = f32[768,96]{0,1:T(8,128)} async-done(((f32[768,1536]{0,1:T(8,128)}), f32[768,96]{0,1:T(8,128)}) %reduce-scatter.43.cloned.1.call-update) | async-done | bytes 294928 | tf_op jit(solution)/shard_map/reduce_scatter | solution.py:318
  2647.8 78.9 %reduce-scatter.41.cloned.1.call-done = f32[96,768]{1,0:T(8,128)} async-done(((f32[1536,768]{1,0:T(8,128)}), f32[96,768]{1,0:T(8,128)}) %reduce-scatter.41.cloned.1.call-update) | async-done | bytes 294928 | tf_op jit(solution)/shard_map/reduce_scatter | solution.py:317
  2726.7 79.6 %reduce-scatter.39.cloned.1.call-done = f32[96,768]{1,0:T(8,128)} async-done(((f32[1536,768]{1,0:T(8,128)}), f32[96,768]{1,0:T(8,128)}) %reduce-scatter.39.cloned.1.call-update) | async-done | bytes 294928 | tf_op jit(solution)/shard_map/reduce_scatter | solution.py:316
  2806.4 79.0 %reduce-scatter.37.cloned.1.call-done = f32[96,768]{1,0:T(8,128)} async-done(((f32[1536,768]{1,0:T(8,128)}), f32[96,768]{1,0:T(8,128)}) %reduce-scatter.37.cloned.1.call-update) | async-done | bytes 294928 | tf_op jit(solution)/shard_map/reduce_scatter | solution.py:315
  (359 shorter events, 276.3 us)
Async XLA Ops:
  7.2 346.6 %copy-start = (bf16[1,130,1536]{2,1,0:T(8,128)(2,1)S(1)}, bf16[1,130,1536]{2,1,0:T(8,128)(2,1)}, u32[]{:S(2)}) copy-start(bf16[1,130,1536]{2,1,0:T(8,128)(2,1)} %param.17) | copy-start | bytes 1198084
  7.2 62.2 %all-gather.18.cloned.1.call-start = ((), (), s32[]{:S(2)}) async-start(), calls=%async_computation.18 | async-start | bytes 3538944 | tf_op jit(solution)/shard_map/all_gather | solution.py:180
  10.6 108.0 %copy-start.69 = (f32[384]{0:T(512)}, f32[384]{0:T(512)S(1)}, u32[]{:S(2)}) copy-start(f32[384]{0:T(512)S(1)} %add_rsqrt_fusion.2) | copy-start | bytes 4612
  33.9 277.7 %copy-start.59 = (f32[1536]{0:T(1024)}, f32[1536]{0:T(1024)S(1)}, u32[]{:S(2)}) copy-start(f32[1536]{0:T(1024)S(1)} %get-tuple-element.91) | copy-start | bytes 18436
  33.9 556.8 %copy-start.61 = (f32[1536]{0:T(1024)}, f32[1536]{0:T(1024)S(1)}, u32[]{:S(2)}) copy-start(f32[1536]{0:T(1024)S(1)} %get-tuple-element.90) | copy-start | bytes 18436
  35.9 78.2 %all-gather.24.cloned.1.call-start = ((), (), s32[]{:S(2)}) async-start(), calls=%async_computation.21 | async-start | bytes 2506752 | tf_op jit(solution)/shard_map/all_gather | solution.py:162
  36.7 120.8 %all-gather.22.cloned.1.call-start = ((), (), s32[]{:S(2)}) async-start(), calls=%async_computation.20 | async-start | bytes 2506752 | tf_op jit(solution)/shard_map/all_gather | solution.py:161
  37.4 163.4 %all-gather.20.cloned.1.call-start = ((), (), s32[]{:S(2)}) async-start(), calls=%async_computation.19 | async-start | bytes 2506752 | tf_op jit(solution)/shard_map/all_gather | solution.py:163
  38.0 206.1 %all-gather.26.cloned.1.call-start = ((), (), s32[]{:S(2)}) async-start(), calls=%async_computation.22 | async-start | bytes 2506752 | tf_op jit(solution)/shard_map/all_gather | solution.py:164
  38.6 270.3 %reduce-scatter.25.cloned.1.call-start = ((), (), s32[]{:S(2)}) async-start(), calls=%async_computation.23 | async-start | bytes 7077888 | tf_op jit(solution)/shard_map/reduce_scatter | solution.py:183
  39.1 122.9 %copy-start.44 = (f32[768,32]{0,1:T(8,128)}, f32[768,32]{0,1:T(8,128)S(1)}, u32[]{:S(2)}) copy-start(f32[768,32]{0,1:T(8,128)S(1)} %get-tuple-element.126) | copy-start | bytes 294916
  39.1 122.9 %copy-start.46 = (f32[768,32]{0,1:T(8,128)}, f32[768,32]{0,1:T(8,128)S(1)}, u32[]{:S(2)}) copy-start(f32[768,32]{0,1:T(8,128)S(1)} %get-tuple-element.127) | copy-start | bytes 294916
  249.9 103.8 %all-gather.28.cloned.1.call-start = ((), (), s32[]{:S(2)}) async-start(), calls=%async_computation.24 | async-start | bytes 2506752 | tf_op jit(solution)/shard_map/all_gather | solution.py:167
  250.7 146.7 %all-gather.34.cloned.1.call-start = ((), (), s32[]{:S(2)}) async-start(), calls=%async_computation.27 | async-start | bytes 2506752 | tf_op jit(solution)/shard_map/all_gather | solution.py:166
  251.4 189.7 %all-gather.32.cloned.1.call-start = ((), (), s32[]{:S(2)}) async-start(), calls=%async_computation.26 | async-start | bytes 2506752 | tf_op jit(solution)/shard_map/all_gather | solution.py:165
  252.2 225.9 %all-gather.30.cloned.1.call-start = ((), (), s32[]{:S(2)}) async-start(), calls=%async_computation.25 | async-start | bytes 3538944 | tf_op jit(solution)/shard_map/all_gather | solution.py:180
  311.2 276.9 %copy-start.2 = (f32[384,1536]{1,0:T(8,128)}, f32[384,1536]{1,0:T(8,128)S(1)}, u32[]{:S(2)}) copy-start(f32[384,1536]{1,0:T(8,128)S(1)} %get-tuple-element.102) | copy-start | bytes 7077892
  313.0 209.9 %all-gather.36.cloned.1.call-start = ((), (), s32[]{:S(2)}) async-start(), calls=%async_computation.28 | async-start | bytes 2506752 | tf_op jit(solution)/shard_map/all_gather | solution.py:168
  313.8 274.3 %reduce-scatter.27.cloned.1.call-start = ((), (), s32[]{:S(2)}) async-start(), calls=%async_computation.29 | async-start | bytes 7077888 | tf_op jit(solution)/shard_map/reduce_scatter | solution.py:183
  399.8 82.7 %copy-start.33 = (bf16[130,768]{0,1:T(8,128)(2,1)}, bf16[130,768]{0,1:T(8,128)(2,1)S(1)}, u32[]{:S(2)}) copy-start(bf16[130,768]{0,1:T(8,128)(2,1)S(1)} %copy.90) | copy-start | bytes 599044
  529.2 472.0 %all-gather.38.cloned.1.call-start = ((), (), s32[]{:S(2)}) async-start(), calls=%async_computation.30 | async-start | bytes 3538944 | tf_op jit(solution)/shard_map/all_gather | solution.py:180
  593.1 421.1 %all-gather.40.cloned.1.call-start = ((), (), s32[]{:S(2)}) async-start(), calls=%async_computation.31 | async-start | bytes 10027008 | tf_op jit(solution)/shard_map/all_gather | solution.py:175
  593.7 436.8 %all-gather.42.cloned.1.call-start = ((), (), s32[]{:S(2)}) async-start(), calls=%async_computation.32 | async-start | bytes 10027008 | tf_op jit(solution)/shard_map/all_gather | solution.py:176
  593.7 2.1 collective-permute-start
  594.3 509.6 %reduce-scatter.29.cloned.1.call-start = ((), (), s32[]{:S(2)}) async-start(), calls=%async_computation.33 | async-start | bytes 7077888 | tf_op jit(solution)/shard_map/reduce_scatter | solution.py:183
  597.0 28.2 collective-permute-start.1
  626.8 100.1 %collective-permute-start.2 = (bf16[4,96,3072]{2,1,0:T(8,128)(2,1)S(1)}, bf16[4,96,3072]{2,1,0:T(8,128)(2,1)}, u32[]{:S(2)}, u32[]{:S(2)}) collective-permute-start(bf16[4,96,3072]{2,1,0:T(8,128)(2,1)S(1)} %pad_maximum_fusion.2), channel_id=1, source_target_pairs={{0,8},{2,10},{4,12},{6,14},{8,0},{10,2},{12,4},{14,6},{16,24},{18,... | collective-permute-start | bytes 7077896 | tf_op jit(solution)/shard_map/ppermute | solution.py:25
  732.5 261.2 %collective-permute-start.3 = (bf16[8,96,3072]{2,1,0:T(8,128)(2,1)}, bf16[8,96,3072]{2,1,0:T(8,128)(2,1)}, u32[]{:S(2)}, u32[]{:S(2)}) collective-permute-start(bf16[8,96,3072]{2,1,0:T(8,128)(2,1)} %pad_maximum_fusion.1), channel_id=1, source_target_pairs={{0,16},{2,18},{4,20},{6,22},{8,24},{10,26},{12,28},{14,30},{16,0},... | collective-permute-start | bytes 14155784 | tf_op jit(solution)/shard_map/ppermute | solution.py:25
  1043.6 100.0 %all-gather.44.cloned.1.call-start = ((), (), s32[]{:S(2)}) async-start(), calls=%async_computation.34 | async-start | bytes 3538944 | tf_op jit(solution)/shard_map/all_gather | solution.py:186
  1107.5 140.1 %reduce-scatter.31.cloned.1.call-start = ((), (), s32[]{:S(2)}) async-start(), calls=%async_computation.35 | async-start | bytes 7077888 | tf_op jit(solution)/shard_map/reduce_scatter | solution.py:189
  1187.5 104.6 %all-gather.46.cloned.1.call-start = ((), (), s32[]{:S(2)}) async-start(), calls=%async_computation.36 | async-start | bytes 3538944 | tf_op jit(solution)/shard_map/all_gather | solution.py:186
  1255.8 114.0 %reduce-scatter.33.cloned.1.call-start = ((), (), s32[]{:S(2)}) async-start(), calls=%async_computation.37 | async-start | bytes 7077888 | tf_op jit(solution)/shard_map/reduce_scatter | solution.py:189
  1309.7 102.2 %all-gather.48.cloned.1.call-start = ((), (), s32[]{:S(2)}) async-start(), calls=%async_computation.38 | async-start | bytes 3538944 | tf_op jit(solution)/shard_map/all_gather | solution.py:186
  1375.6 188.3 %reduce-scatter.35.cloned.1.call-start = ((), (), s32[]{:S(2)}) async-start(), calls=%async_computation.39 | async-start | bytes 7077888 | tf_op jit(solution)/shard_map/reduce_scatter | solution.py:189
  1428.2 71.3 %copy-start.28 = (bf16[12,64,768]{2,1,0:T(8,128)(2,1)}, bf16[12,64,768]{2,1,0:T(8,128)(2,1)S(1)}, u32[]{:S(2)}) copy-start(bf16[12,64,768]{2,1,0:T(8,128)(2,1)S(1)} %fusion.33) | copy-start | bytes 3538948
  1503.7 216.9 %all-reduce.2.cloned.1.call-start = ((), (), s32[]{:S(2)}) async-start(), calls=%async_computation.40 | async-start | bytes 835584 | tf_op jit(solution)/shard_map/psum | solution.py:301
  1515.0 212.8 %reduce-scatter.59.cloned.1.call-start = ((), (), s32[]{:S(2)}) async-start(), calls=%async_computation.52 | async-start | bytes 835584
  1574.6 158.7 %reduce-scatter.47.cloned.1.call-start = ((), (), s32[]{:S(2)}) async-start(), calls=%async_computation.46 | async-start | bytes 5013504 | tf_op jit(solution)/shard_map/reduce_scatter | solution.py:322
  1580.9 231.3 %reduce-scatter.45.cloned.1.call-start = ((), (), s32[]{:S(2)}) async-start(), calls=%async_computation.45 | async-start | bytes 5013504 | tf_op jit(solution)/shard_map/reduce_scatter | solution.py:319
  1587.1 304.5 %reduce-scatter.57.cloned.1.call-start = ((), (), s32[]{:S(2)}) async-start(), calls=%async_computation.51 | async-start | bytes 5013504
  1596.2 374.5 %reduce-scatter.55.cloned.1.call-start = ((), (), s32[]{:S(2)}) async-start(), calls=%async_computation.50 | async-start | bytes 5013504
  1605.5 564.4 %reduce-scatter.53.cloned.1.call-start = ((), (), s32[]{:S(2)}) async-start(), calls=%async_computation.49 | async-start | bytes 20054016 | tf_op jit(solution)/shard_map/reduce_scatter | solution.py:253
  1620.1 748.9 %reduce-scatter.49.cloned.1.call-start = ((), (), s32[]{:S(2)}) async-start(), calls=%async_computation.47 | async-start | bytes 20054016 | tf_op jit(solution)/shard_map/reduce_scatter | solution.py:251
  1634.1 934.1 %reduce-scatter.51.cloned.1.call-start = ((), (), s32[]{:S(2)}) async-start(), calls=%async_computation.48 | async-start | bytes 20054016 | tf_op jit(solution)/shard_map/reduce_scatter | solution.py:252
  1647.9 999.9 %reduce-scatter.43.cloned.1.call-start = ((), (), s32[]{:S(2)}) async-start(), calls=%async_computation.44 | async-start | bytes 5013504 | tf_op jit(solution)/shard_map/reduce_scatter | solution.py:318
  1655.2 1071.5 %reduce-scatter.41.cloned.1.call-start = ((), (), s32[]{:S(2)}) async-start(), calls=%async_computation.43 | async-start | bytes 5013504 | tf_op jit(solution)/shard_map/reduce_scatter | solution.py:317
  1662.4 1144.0 %reduce-scatter.39.cloned.1.call-start = ((), (), s32[]{:S(2)}) async-start(), calls=%async_computation.42 | async-start | bytes 5013504 | tf_op jit(solution)/shard_map/reduce_scatter | solution.py:316
  1669.8 1215.6 %reduce-scatter.37.cloned.1.call-start = ((), (), s32[]{:S(2)}) async-start(), calls=%async_computation.41 | async-start | bytes 5013504 | tf_op jit(solution)/shard_map/reduce_scatter | solution.py:315
  (81 other events, 1237.1 us)
Sparse Core Ops, SparseCore 0:
  36.0 33.3 all-gather.17
  71.7 42.3 all-gather.23
  116.4 41.0 all-gather.21
  159.7 41.0 all-gather.19
  202.9 41.0 all-gather.25
  250.1 58.7 reduce-scatter.24
  311.4 42.3 all-gather.27
  356.3 41.0 all-gather.33
  400.0 41.0 all-gather.31
  443.2 34.8 all-gather.29
  480.6 42.3 all-gather.35
  529.3 58.7 reduce-scatter.26
  593.2 36.0 all-gather.37
  631.5 109.6 all-gather.39
  743.3 191.0 all-gather.41
  1043.7 60.1 reduce-scatter.28
  1107.6 35.9 all-gather.43
  1187.6 59.9 reduce-scatter.30
  1255.9 36.0 all-gather.45
  1309.8 59.9 reduce-scatter.32
  1375.7 36.0 all-gather.47
  1503.8 59.9 reduce-scatter.34
  1566.7 26.2 all-reduce.1
  1596.5 56.6 reduce-scatter.58
  1658.1 75.1 reduce-scatter.46
  1737.6 74.5 reduce-scatter.44
  1817.0 74.6 reduce-scatter.56
  1896.1 74.5 reduce-scatter.54
  1976.0 193.8 reduce-scatter.52
  2174.9 194.0 reduce-scatter.48
  2374.3 193.8 reduce-scatter.50
  2573.1 74.6 reduce-scatter.42
  2652.1 74.6 reduce-scatter.40
  2731.7 74.6 reduce-scatter.38
  2810.8 74.5 reduce-scatter.36
